TPU v7x, 256 devices: a whole 4x4x8 slice. The times are simulated.
256 devices in a mesh: seq: 64 (over y, z, core), tp: 4 (over x).
Axes of the slice: x: 4, y: 4, z: 8, core: 2. Of those that a mesh axis runs over, the one named last changes fastest.
Arguments:
- inputs: bfloat16 [4, 4, 1024], P(None, None, 'tp'), may hold values from -64 to 64
- attention_gain: bfloat16 [1024], replicated, may hold values from 0.099609375 to 1.8984375
- forward_gain: bfloat16 [1024], replicated, may hold values from 0.099609375 to 1.8984375
- query_weight: bfloat16 [1024, 1024], P(None, 'tp'), may hold values from -0.1875 to 0.1875
- key_weight: bfloat16 [1024, 1024], P(None, 'tp'), may hold values from -0.1875 to 0.1875
- value_weight: bfloat16 [1024, 1024], P(None, 'tp'), may hold values from -0.1875 to 0.1875
- output_weight: bfloat16 [1024, 1024], P('tp'), may hold values from -0.1875 to 0.1875
- gate_weight: bfloat16 [1024, 4096], P(None, 'tp'), may hold values from -0.1875 to 0.1875
- up_weight: bfloat16 [1024, 4096], P(None, 'tp'), may hold values from -0.1875 to 0.1875
- down_weight: bfloat16 [4096, 1024], P('tp'), may hold values from -0.09375 to 0.09375
- variate_bias: float32 [2, 16], replicated, may hold values from -256 to 256
- cache_keys: bfloat16 [4, 32768, 1024], P(None, 'seq', 'tp'), may hold values from -15 to 15
- cache_values: bfloat16 [4, 32768, 1024], P(None, 'seq', 'tp'), may hold values from -12 to 12
- cache_variates: int32 [4, 32768], P(None, 'seq'), may hold values from 0 to 7
- cache_mask: int32 [4, 32768], P(None, 'seq'), may hold values 0 or 1
- cache_lengths: int32 [4], replicated, may hold values from 1 to 32768, as said below
- fresh_flags: int32 [4], replicated, may hold values 0 or 1
- new_variates: int32 [4, 4], replicated, may hold values from 0 to 7
- new_times: int32 [4, 4], replicated, may hold values from 0 to 32771
Outputs:
- hidden_states: bfloat16 [4, 4, 1024], P(None, None, 'tp')
- new_keys: bfloat16 [4, 4, 1024], P(None, None, 'tp')
- new_values: bfloat16 [4, 4, 1024], P(None, None, 'tp')
Inputs may be any that keep to these rules, and one draw needn't show every extreme that they name: `cache_lengths`: some request has exactly 32768 filled positions.
All inputs are finite; a program needn't handle non-finite values. No bound on the sum of `cache_mask` on one device may be relied on, other than what follows from the above.
Results may differ from a plain program's by a relative error of at most 0.014.
Values may be sent and summed in bfloat16 or wider, within the bound.
A program may use at most 64 MiB of HBM per device.

v0:
```python
import math
import jax
import jax.numpy as jnp
from jax import lax
from jax.sharding import PartitionSpec as P

D = 1024
HEAD_DIM = 64
STEPS = 4
epsilon = 1e-05


def rotated(blocks, times):
    half = blocks.shape[-1] // 2
    ladder = jnp.arange(half, dtype=jnp.float32) * (2.0 / blocks.shape[-1])
    inverse = jnp.exp(-math.log(10000.0) * ladder)
    angles = times.astype(jnp.float32)[:, None] * inverse[None, :]
    cosine = jnp.cos(angles)[:, None, :]
    sine = jnp.sin(angles)[:, None, :]
    first = blocks[..., :half]
    second = blocks[..., half:]
    return jnp.concatenate(
        [first * cosine - second * sine, second * cosine + first * sine], axis=-1
    )


def join_parts(earlier, later):
    peak = jnp.maximum(earlier[0], later[0])
    factor_one = jnp.exp(earlier[0] - peak)
    factor_two = jnp.exp(later[0] - peak)
    totals = earlier[1] * factor_one + later[1] * factor_two
    repeat_by = earlier[2].shape[-1] // earlier[0].shape[-1]
    sums = earlier[2] * jnp.repeat(factor_one, repeat_by, axis=1) + later[2] * jnp.repeat(
        factor_two, repeat_by, axis=1
    )
    return (peak, totals, sums)


def on_device(
    inputs,
    attention_gain,
    forward_gain,
    query_weight,
    key_weight,
    value_weight,
    output_weight,
    gate_weight,
    up_weight,
    down_weight,
    variate_bias,
    cache_keys,
    cache_values,
    cache_variates,
    cache_mask,
    cache_lengths,
    fresh_flags,
    new_variates,
    new_times,
):
    local_width = query_weight.shape[1]
    local_heads = local_width // HEAD_DIM
    requests = inputs.shape[0]
    columns = inputs.shape[2]
    span = cache_keys.shape[1]
    scale = 1.0 / math.sqrt(HEAD_DIM)
    column_start = lax.axis_index("tp") * columns
    head_start = lax.axis_index("tp") * local_heads
    bias_local = lax.dynamic_slice_in_dim(variate_bias, head_start, local_heads, 1)
    same_bias = bias_local[0]
    other_bias = bias_local[1]
    positions = lax.axis_index("seq") * span + jnp.arange(span, dtype=jnp.int32)
    usable = (
        (positions[None, :] < cache_lengths[:, None])
        & (cache_mask == 1)
        & (fresh_flags[:, None] == 0)
    )
    key_blocks = cache_keys.reshape(requests, span, local_heads, HEAD_DIM)
    value_blocks = cache_values.reshape(requests, span, local_heads, HEAD_DIM)
    gain_first = attention_gain.astype(jnp.float32)[None, :]
    gain_second = forward_gain.astype(jnp.float32)[None, :]
    gain_first_local = lax.dynamic_slice_in_dim(gain_first, column_start, columns, 1)
    gain_second_local = lax.dynamic_slice_in_dim(gain_second, column_start, columns, 1)
    hidden_list = []
    key_list = []
    value_list = []
    for step_index in range(STEPS):
        current_low = inputs[:, step_index, :]
        current_local = current_low.astype(jnp.float32)
        square_sum = lax.psum(jnp.sum(current_local * current_local, axis=1), "tp")
        inverse_rms = lax.rsqrt(square_sum / D + epsilon)
        normed_local = (current_local * inverse_rms[:, None] * gain_first_local).astype(
            jnp.bfloat16
        )
        normed = lax.all_gather(normed_local, "tp", axis=1, tiled=True)
        query_full = jnp.dot(normed, query_weight, preferred_element_type=jnp.float32)
        key_full = jnp.dot(normed, key_weight, preferred_element_type=jnp.float32)
        value_full = jnp.dot(normed, value_weight, preferred_element_type=jnp.float32)
        times_now = new_times[:, step_index]
        queries_now = rotated(
            query_full.reshape(requests, local_heads, HEAD_DIM), times_now
        ).astype(jnp.bfloat16)
        keys_now = rotated(key_full.reshape(requests, local_heads, HEAD_DIM), times_now).astype(
            jnp.bfloat16
        )
        values_now = value_full.reshape(requests, local_heads, HEAD_DIM).astype(jnp.bfloat16)
        key_list.append(keys_now)
        value_list.append(values_now)
        variate_now = new_variates[:, step_index]
        same_cache = cache_variates == variate_now[:, None]
        scores = (
            jnp.einsum("rhe,rche->rhc", queries_now, key_blocks, preferred_element_type=jnp.float32)
            * scale
        )
        scores = scores + jnp.where(
            same_cache[:, None, :], same_bias[None, :, None], other_bias[None, :, None]
        )
        scores = jnp.where(usable[:, None, :], scores, -1e30)
        local_peak = jnp.max(scores, axis=2)
        raw = jnp.where(usable[:, None, :], jnp.exp(scores - local_peak[:, :, None]), 0.0)
        local_total = jnp.sum(raw, axis=2)
        local_sum = jnp.einsum(
            "rhc,rche->rhe",
            raw.astype(jnp.bfloat16),
            value_blocks,
            preferred_element_type=jnp.float32,
        ).reshape(requests, local_width)
        peak_all = lax.pmax(local_peak, "seq")
        factor = jnp.exp(local_peak - peak_all)
        totals_all, sums_all = lax.psum(
            (local_total * factor, local_sum * jnp.repeat(factor, HEAD_DIM, axis=1)), "seq"
        )
        merged = (peak_all, totals_all, sums_all)
        fresh_keys = jnp.stack(key_list, axis=1)
        fresh_values = jnp.stack(value_list, axis=1)
        same_new = new_variates[:, : step_index + 1] == variate_now[:, None]
        new_scores = (
            jnp.einsum("rhe,rshe->rhs", queries_now, fresh_keys, preferred_element_type=jnp.float32)
            * scale
        )
        new_scores = new_scores + jnp.where(
            same_new[:, None, :], same_bias[None, :, None], other_bias[None, :, None]
        )
        new_peak = jnp.max(new_scores, axis=2)
        new_raw = jnp.exp(new_scores - new_peak[:, :, None])
        new_total = jnp.sum(new_raw, axis=2)
        new_sum = jnp.einsum(
            "rhs,rshe->rhe",
            new_raw.astype(jnp.bfloat16),
            fresh_values,
            preferred_element_type=jnp.float32,
        ).reshape(requests, local_width)
        joined = join_parts(merged, (new_peak, new_total, new_sum))
        attention = (joined[2] / jnp.repeat(joined[1], HEAD_DIM, axis=1)).astype(jnp.bfloat16)
        partial_out = jnp.dot(attention, output_weight, preferred_element_type=jnp.float32)
        projected_local = lax.psum_scatter(partial_out, "tp", scatter_dimension=1, tiled=True)
        middle_local = (current_local + projected_local).astype(jnp.bfloat16).astype(jnp.float32)
        middle_sum = lax.psum(jnp.sum(middle_local * middle_local, axis=1), "tp")
        second_rms = lax.rsqrt(middle_sum / D + epsilon)
        normed_two_local = (middle_local * second_rms[:, None] * gain_second_local).astype(
            jnp.bfloat16
        )
        normed_two = lax.all_gather(normed_two_local, "tp", axis=1, tiled=True)
        gate_part = jnp.dot(normed_two, gate_weight, preferred_element_type=jnp.float32)
        up_part = jnp.dot(normed_two, up_weight, preferred_element_type=jnp.float32)
        activated = (jax.nn.silu(gate_part) * up_part).astype(jnp.bfloat16)
        down_part = jnp.dot(activated, down_weight, preferred_element_type=jnp.float32)
        forward = lax.psum_scatter(down_part, "tp", scatter_dimension=1, tiled=True)
        hidden_list.append((middle_local + forward).astype(jnp.bfloat16))
    hidden_states = jnp.stack(hidden_list, axis=1)
    new_keys = jnp.stack(key_list, axis=1).reshape(requests, STEPS, local_width)
    new_values = jnp.stack(value_list, axis=1).reshape(requests, STEPS, local_width)
    return (hidden_states, new_keys, new_values)


def solution(mesh):
    return jax.shard_map(
        on_device,
        mesh=mesh,
        in_specs=(
            P(None, None, "tp"),
            P(),
            P(),
            P(None, "tp"),
            P(None, "tp"),
            P(None, "tp"),
            P("tp", None),
            P(None, "tp"),
            P(None, "tp"),
            P("tp", None),
            P(),
            P(None, "seq", "tp"),
            P(None, "seq", "tp"),
            P(None, "seq"),
            P(None, "seq"),
            P(),
            P(),
            P(),
            P(),
        ),
        out_specs=(P(None, None, "tp"), P(None, None, "tp"), P(None, None, "tp")),
        check_vma=False,
    )
```

profile of v0, /device:TPU:8, one launch (start us, length us, event | category | flops | bytes accessed | tf_op | source)
XLA Modules:
  0.0 712.5 jit_solution(17226373592038998446)
XLA Ops:
  7.3 0.9 fusion.172
  8.7 10.5 %all-reduce.3 = (f32[4]{0:T(128)S(1)}, f32[4]{0:T(128)S(1)}, f32[4]{0:T(128)S(1)}, f32[4]{0:T(128)S(1)}) all-reduce(f32[4]{0:T(128)S(1)} %fusion.94, f32[4]{0:T(128)S(1)} %fusion.106, f32[4]{0:T(128)S(1)} %fusion.102, f32[4]{0:T(128)S(1)} %fusion.98), channel_id=1, replica_groups=mesh['seq'=64,'tp'=4] {'tp'}, use_global_device_ids=true, to_apply=%region_1.0 | all-reduce | flops 16 | bytes 128 | tf_op jit(solution)/shard_map/psum | solution.py:89
  19.2 0.8 dynamic-slice.6
  20.1 10.4 %all_gather.24 = bf16[4,1024]{1,0:T(4,128)(2,1)S(1)} all-gather(bf16[4,256]{1,0:T(4,128)(2,1)S(1)} %get-tuple-element.136), channel_id=1, replica_groups=mesh['seq'=64,'tp'=4] {'tp'}, dimensions={1}, use_global_device_ids=true | all-gather | bytes 10240 | tf_op jit(solution)/shard_map/all_gather | solution.py:94
  30.5 1.2 convolution_convert_fusion.3
  31.7 1.2 fusion.174
  32.9 10.5 %all_gather.26 = bf16[4,1024]{1,0:T(4,128)(2,1)S(1)} all-gather(bf16[4,256]{1,0:T(4,128)(2,1)S(1)} %get-tuple-element.137), channel_id=1, replica_groups=mesh['seq'=64,'tp'=4] {'tp'}, dimensions={1}, use_global_device_ids=true | all-gather | bytes 10240 | tf_op jit(solution)/shard_map/all_gather | solution.py:94
  43.4 1.2 convolution_convert_fusion.2
  44.6 1.2 fusion.177
  46.2 10.4 %all_gather.28 = bf16[4,1024]{1,0:T(4,128)(2,1)S(1)} all-gather(bf16[4,256]{1,0:T(4,128)(2,1)S(1)} %get-tuple-element.138), channel_id=1, replica_groups=mesh['seq'=64,'tp'=4] {'tp'}, dimensions={1}, use_global_device_ids=true | all-gather | bytes 10240 | tf_op jit(solution)/shard_map/all_gather | solution.py:94
  57.1 10.5 %all_gather.30 = bf16[4,1024]{1,0:T(4,128)(2,1)S(1)} all-gather(bf16[4,256]{1,0:T(4,128)(2,1)S(1)} %get-tuple-element.139), channel_id=1, replica_groups=mesh['seq'=64,'tp'=4] {'tp'}, dimensions={1}, use_global_device_ids=true | all-gather | bytes 10240 | tf_op jit(solution)/shard_map/all_gather | solution.py:94
  70.6 1.5 copy.47
  73.9 1.5 copy.48
  75.8 108.2 %all-reduce.1 = (f32[4,4]{1,0:T(4,128)S(1)}, f32[4,4]{1,0:T(4,128)S(1)}, f32[4,4]{1,0:T(4,128)S(1)}, f32[4,4]{1,0:T(4,128)S(1)}) all-reduce(f32[4,4]{1,0:T(4,128)S(1)} %get-tuple-element.78, f32[4,4]{1,0:T(4,128)S(1)} %get-tuple-element.125, f32[4,4]{1,0:T(4,128)S(1)} %get-tuple-element.123, ...), channel_id=1, replica_groups=mesh['seq'=64,'tp'=4] {'seq'}, use_global_device_ids=true, to_apply=%region_40.41 | all-reduce | flops 64 | bytes 512 | tf_op jit(solution)/shard_map/pmax | solution.py:127
  184.6 1.7 fusion.14
  186.3 1.6 fusion.16
  189.5 231.8 %all-reduce = (f32[4,4]{1,0:T(4,128)S(1)}, f32[4,256]{1,0:T(4,128)S(1)}, f32[4,4]{1,0:T(4,128)S(1)}, f32[4,256]{1,0:T(4,128)S(1)}, f32[4,4]{1,0:T(4,128)S(1)}, /...) all-reduce(f32[4,4]{1,0:T(4,128)S(1)} %get-tuple-element.70, ...), channel_id=1, replica_groups=mesh['seq'=64,'tp'=4] {'seq'}, use_global_device_ids=true, to_apply=%region_44.45 | all-reduce | flops 4160 | bytes 33280 | tf_op jit(solution)/shard_map/psum | solution.py:129
  421.8 1.2 convolution_bitcast_fusion.4
  424.5 1.2 convolution_bitcast_fusion.5
  427.2 1.2 convolution_bitcast_fusion.6
  429.2 1.1 convolution_bitcast_fusion.7
  430.8 0.6 copy.56
  432.0 43.5 %reduce-scatter.37.cloned.1.call-done = f32[256,4]{1,0:T(8,128)} async-done(((f32[1024,4]{1,0:T(8,128)}), f32[256,4]{1,0:T(8,128)}) %reduce-scatter.37.cloned.1.call-update) | async-done | bytes 4112
  475.5 1.0 copy.105
  476.5 25.3 %reduce-scatter.33.cloned.1.call-done = f32[256,4]{1,0:T(8,128)} async-done(((f32[1024,4]{1,0:T(8,128)}), f32[256,4]{1,0:T(8,128)}) %reduce-scatter.33.cloned.1.call-update) | async-done | bytes 4112
  501.8 1.0 copy.101
  502.7 25.3 %reduce-scatter.29.cloned.1.call-done = f32[256,4]{1,0:T(8,128)} async-done(((f32[1024,4]{1,0:T(8,128)}), f32[256,4]{1,0:T(8,128)}) %reduce-scatter.29.cloned.1.call-update) | async-done | bytes 4112
  528.1 1.0 copy.97
  529.0 25.2 %reduce-scatter.25.cloned.1.call-done = f32[256,4]{1,0:T(8,128)} async-done(((f32[1024,4]{1,0:T(8,128)}), f32[256,4]{1,0:T(8,128)}) %reduce-scatter.25.cloned.1.call-update) | async-done | bytes 4112
  554.2 1.0 copy.93
  555.5 8.4 %all-reduce.2 = (f32[4]{0:T(128)S(1)}, f32[4]{0:T(128)S(1)}, f32[4]{0:T(128)S(1)}, f32[4]{0:T(128)S(1)}) all-reduce(f32[4]{0:T(128)S(1)} %get-tuple-element.156, f32[4]{0:T(128)S(1)} %get-tuple-element.54, f32[4]{0:T(128)S(1)} %get-tuple-element.154, f32[4]{0:T(128)S(1)} %get-tuple-element.47), channel_id=1, replica_groups=mesh['seq'=64,'tp'=4] {'tp'}, use_global_device_ids=true, to_apply=%region_48.49 | all-reduce | flops 16 | bytes 128 | tf_op jit(solution)/shard_map/psum | solution.py:157
  564.0 10.4 %all_gather.25 = bf16[4,1024]{1,0:T(4,128)(2,1)S(1)} all-gather(bf16[4,256]{1,0:T(4,128)(2,1)S(1)} %get-tuple-element.130), channel_id=1, replica_groups=mesh['seq'=64,'tp'=4] {'tp'}, dimensions={1}, use_global_device_ids=true | all-gather | bytes 10240 | tf_op jit(solution)/shard_map/all_gather | solution.py:162
  574.4 10.4 %all_gather.27 = bf16[4,1024]{1,0:T(4,128)(2,1)S(1)} all-gather(bf16[4,256]{1,0:T(4,128)(2,1)S(1)} %get-tuple-element.131), channel_id=1, replica_groups=mesh['seq'=64,'tp'=4] {'tp'}, dimensions={1}, use_global_device_ids=true | all-gather | bytes 10240 | tf_op jit(solution)/shard_map/all_gather | solution.py:162
  584.8 10.4 %all_gather.29 = bf16[4,1024]{1,0:T(4,128)(2,1)S(1)} all-gather(bf16[4,256]{1,0:T(4,128)(2,1)S(1)} %get-tuple-element.132), channel_id=1, replica_groups=mesh['seq'=64,'tp'=4] {'tp'}, dimensions={1}, use_global_device_ids=true | all-gather | bytes 10240 | tf_op jit(solution)/shard_map/all_gather | solution.py:162
  596.3 4.1 convolution_bitcast_fusion.3
  600.7 4.1 convolution_bitcast_fusion.2
  604.8 4.1 convolution_bitcast_fusion.1
  608.8 10.5 %all_gather.31 = bf16[4,1024]{1,0:T(4,128)(2,1)S(1)} all-gather(bf16[4,256]{1,0:T(4,128)(2,1)S(1)} %get-tuple-element.133), channel_id=1, replica_groups=mesh['seq'=64,'tp'=4] {'tp'}, dimensions={1}, use_global_device_ids=true | all-gather | bytes 10240 | tf_op jit(solution)/shard_map/all_gather | solution.py:162
  620.1 4.1 convolution_bitcast_fusion
  624.2 1.1 reduce-scatter.27.cloned.1.call-done
  625.3 1.0 copy.95
  626.3 25.2 %reduce-scatter.31.cloned.1.call-done = f32[256,4]{1,0:T(8,128)} async-done(((f32[1024,4]{1,0:T(8,128)}), f32[256,4]{1,0:T(8,128)}) %reduce-scatter.31.cloned.1.call-update) | async-done | bytes 4112
  651.5 1.0 copy.99
  652.4 25.3 %reduce-scatter.35.cloned.1.call-done = f32[256,4]{1,0:T(8,128)} async-done(((f32[1024,4]{1,0:T(8,128)}), f32[256,4]{1,0:T(8,128)}) %reduce-scatter.35.cloned.1.call-update) | async-done | bytes 4112
  677.7 1.0 copy.103
  678.7 25.3 %reduce-scatter.39.cloned.1.call-done = f32[256,4]{1,0:T(8,128)} async-done(((f32[1024,4]{1,0:T(8,128)}), f32[256,4]{1,0:T(8,128)}) %reduce-scatter.39.cloned.1.call-update) | async-done | bytes 4112
  704.0 1.0 copy.107
  705.0 0.6 copy.54
  (202 shorter events, 16.8 us)
Async XLA Ops:
  7.2 588.0 %copy-start = (bf16[1024,1024]{1,0:T(8,128)(2,1)S(1)}, bf16[1024,1024]{1,0:T(8,128)(2,1)}, u32[]{:S(2)}) copy-start(bf16[1024,1024]{1,0:T(8,128)(2,1)} %param.26) | copy-start | bytes 6291460
  7.2 49.4 %copy-start.1 = (bf16[1024,256]{1,0:T(8,128)(2,1)S(1)}, bf16[1024,256]{1,0:T(8,128)(2,1)}, u32[]{:S(2)}) copy-start(bf16[1024,256]{1,0:T(8,128)(2,1)} %param.24) | copy-start | bytes 1572868
  7.2 49.6 %copy-start.2 = (bf16[1024,256]{1,0:T(8,128)(2,1)S(1)}, bf16[1024,256]{1,0:T(8,128)(2,1)}, u32[]{:S(2)}) copy-start(bf16[1024,256]{1,0:T(8,128)(2,1)} %param.23) | copy-start | bytes 1572868
  7.2 468.3 %reduce-scatter.37.cloned.1.call-start = ((), (), s32[]{:S(2)}) async-start(), calls=%async_computation.14 | async-start | bytes 655360
  19.2 26.6 %copy-start.3 = (bf16[1024,256]{1,0:T(8,128)(2,1)S(1)}, bf16[1024,256]{1,0:T(8,128)(2,1)}, u32[]{:S(2)}) copy-start(bf16[1024,256]{1,0:T(8,128)(2,1)} %param.22) | copy-start | bytes 1572868
  45.8 22.3 %copy-start.11 = (f32[2,16]{1,0:T(2,128)S(1)}, f32[2,16]{1,0:T(2,128)}, u32[]{:S(2)}) copy-start(f32[2,16]{1,0:T(2,128)} %param.29) | copy-start | bytes 388
  45.8 22.4 %copy-start.14 = (s32[4]{0:T(128)S(1)}, s32[4]{0:T(128)}, u32[]{:S(2)}) copy-start(s32[4]{0:T(128)} %param.35) | copy-start | bytes 52
  45.8 22.4 %copy-start.8 = (s32[4,4]{1,0:T(4,128)S(1)}, s32[4,4]{1,0:T(4,128)}, u32[]{:S(2)}) copy-start(s32[4,4]{1,0:T(4,128)} %param.37) | copy-start | bytes 196
  45.8 22.6 %copy-start.7 = (s32[4,4]{1,0:T(4,128)S(1)}, s32[4,4]{1,0:T(4,128)}, u32[]{:S(2)}) copy-start(s32[4,4]{1,0:T(4,128)} %param.36) | copy-start | bytes 196
  73.3 2.1 copy-start.10
  73.3 2.1 copy-start.13
  73.3 2.2 copy-start.9
  75.4 108.8 %copy-start.5 = (bf16[4,512,256]{1,2,0:T(8,128)(2,1)}, bf16[4,512,256]{1,2,0:T(8,128)(2,1)S(1)}, u32[]{:S(2)}) copy-start(bf16[4,512,256]{1,2,0:T(8,128)(2,1)S(1)} %copy.48) | copy-start | bytes 3145732
  184.6 3.3 copy-start.6
  184.6 237.2 %copy-start.4 = (bf16[256,1024]{1,0:T(8,128)(2,1)S(1)}, bf16[256,1024]{1,0:T(8,128)(2,1)}, u32[]{:S(2)}) copy-start(bf16[256,1024]{1,0:T(8,128)(2,1)} %param.25) | copy-start | bytes 1572868
  423.0 78.7 %reduce-scatter.33.cloned.1.call-start = ((), (), s32[]{:S(2)}) async-start(), calls=%async_computation.12 | async-start | bytes 655360
  425.7 5.1 copy-start.12
  425.7 102.4 %reduce-scatter.29.cloned.1.call-start = ((), (), s32[]{:S(2)}) async-start(), calls=%async_computation.10 | async-start | bytes 655360
  428.4 125.8 %reduce-scatter.25.cloned.1.call-start = ((), (), s32[]{:S(2)}) async-start(), calls=%async_computation.8 | async-start | bytes 655360
  430.3 195.0 %reduce-scatter.27.cloned.1.call-start = ((), (), s32[]{:S(2)}) async-start(), calls=%async_computation.9 | async-start | bytes 655360
  600.5 51.0 %reduce-scatter.31.cloned.1.call-start = ((), (), s32[]{:S(2)}) async-start(), calls=%async_computation.11 | async-start | bytes 655360
  619.3 58.4 %reduce-scatter.35.cloned.1.call-start = ((), (), s32[]{:S(2)}) async-start(), calls=%async_computation.13 | async-start | bytes 655360
  620.1 84.0 %reduce-scatter.39.cloned.1.call-start = ((), (), s32[]{:S(2)}) async-start(), calls=%async_computation.15 | async-start | bytes 655360
Sparse Core Ops, SparseCore 0:
  423.1 52.3 reduce-scatter.36
  478.1 23.6 reduce-scatter.32
  504.3 23.7 reduce-scatter.28
  530.4 23.7 reduce-scatter.24
  600.6 24.6 reduce-scatter.26
  627.7 23.7 reduce-scatter.30
  654.0 23.7 reduce-scatter.34
  680.3 23.7 reduce-scatter.38
where the time goes:
time: 713 us; the launch traced here: 712 us
  blocking collectives  442 us (62%)
  waiting for transfers between devices  196 us (27%)
  matrix products  34.7 us (5%)
  local copies, waits for them, and re-layouts  18.9 us (3%)
  between operations  14.5 us (2%)
    psum x1, blocking collectives, on_device(): lax.psum((local_total * factor, local_sum * jnp.repeat(factor, HEAD_DIM,...  232 us
    unnamed x16, waiting for transfers between devices  196 us
    pmax x1, blocking collectives, on_device(): peak_all = lax.pmax(local_peak, 'seq')  108 us
    all_gather x4, blocking collectives, on_device(): normed = lax.all_gather(normed_local, 'tp', axis=1, tiled=True)  41.7 us
    all_gather x4, blocking collectives, on_device(): normed_two = lax.all_gather(normed_two_local, 'tp', axis=1, tiled=True)  41.6 us
    unnamed x8, matrix products  21 us
  transfers between devices with their start and end apart: 8, of which 8 were waited for; matrix products, arithmetic and copies ran while one was open for 4% of the time, Pallas kernels for 0%

commit v1 on v0

--- a/solution.py
+++ b/solution.py
@@ -91,7 +91,9 @@
         normed_local = (current_local * inverse_rms[:, None] * gain_first_local).astype(
             jnp.bfloat16
         )
-        normed = lax.all_gather(normed_local, "tp", axis=1, tiled=True)
+        normed = jnp.concatenate(
+            lax.all_to_all(jnp.stack([normed_local] * lax.axis_size("tp")), "tp", 0, 0), axis=1
+        )
         query_full = jnp.dot(normed, query_weight, preferred_element_type=jnp.float32)
         key_full = jnp.dot(normed, key_weight, preferred_element_type=jnp.float32)
         value_full = jnp.dot(normed, value_weight, preferred_element_type=jnp.float32)

time: 713 us -> 719 us (level)
  blocking collectives: 442 us -> 401 us
  starting transfers between devices: 0.51 us -> 15.1 us
  local copies, waits for them, and re-layouts: 18.9 us -> 28.9 us
  waiting for transfers between devices: 196 us -> 206 us
  matrix products: 34.7 us -> 42.7 us
    all_gather x4 -> x0, blocking collectives: 41.7 us -> none  [on_device(): normed = lax.all_gather(normed_local, 'tp', axis=1, tiled=True)]
    all_to_all x0 -> x4, starting transfers between devices: none -> 14.8 us  [on_device(): lax.all_to_all(jnp.stack([normed_local] * lax.axis_size('tp')), 'tp', 0, 0)]
    all_to_all x0 -> x4, waiting for transfers between devices: none -> 7.81 us  [on_device(): lax.all_to_all(jnp.stack([normed_local] * lax.axis_size('tp')), 'tp', 0, 0)]
    unnamed x43 -> x28, local copies, waits for them, and re-layouts: 12.7 us -> 18.6 us
  transfers between devices with their start and end apart: 8 -> 12, of which waited for: 8 -> 11; matrix products, arithmetic and copies ran while one was open for 4% -> 7% of each run, Pallas kernels for 0% -> 0%
where the time goes in v1:
time: 719 us; the launch traced here: 717 us
  blocking collectives  401 us (56%)
  waiting for transfers between devices  206 us (29%)
  matrix products  42.7 us (6%)
  local copies, waits for them, and re-layouts  28.9 us (4%)
  starting transfers between devices  15.1 us (2%)
  between operations  14.5 us (2%)
  other arithmetic  10 us (1%)
    psum x1, blocking collectives, on_device(): lax.psum((local_total * factor, local_sum * jnp.repeat(factor, HEAD_DIM,...  232 us
    unnamed x16, waiting for transfers between devices  198 us
    pmax x1, blocking collectives, on_device(): peak_all = lax.pmax(local_peak, 'seq')  108 us
    all_gather x4, blocking collectives, on_device(): normed_two = lax.all_gather(normed_two_local, 'tp', axis=1, tiled=True)  41.8 us
    unnamed x8, matrix products  21 us
    unnamed x28, local copies, waits for them, and re-layouts  18.6 us
    all_to_all x4, starting transfers between devices, on_device(): lax.all_to_all(jnp.stack([normed_local] * lax.axis_size('tp')), 'tp', 0, 0)  14.8 us
  transfers between devices with their start and end apart: 12, of which 11 were waited for; matrix products, arithmetic and copies ran while one was open for 7% of the time, Pallas kernels for 0%

profile of v1, /device:TPU:8, one launch (start us, length us, event | category | flops | bytes accessed | tf_op | source)
XLA Modules:
  0.0 717.4 jit_solution(16635086544107944688)
XLA Ops:
  8.6 10.5 %all-reduce.3 = (f32[4]{0:T(128)S(1)}, f32[4]{0:T(128)S(1)}, f32[4]{0:T(128)S(1)}, f32[4]{0:T(128)S(1)}) all-reduce(f32[4]{0:T(128)S(1)} %fusion.106, f32[4]{0:T(128)S(1)} %fusion.102, f32[4]{0:T(128)S(1)} %fusion.98, f32[4]{0:T(128)S(1)} %fusion.94), channel_id=1, replica_groups=mesh['seq'=64,'tp'=4] {'tp'}, use_global_device_ids=true, to_apply=%region_38.39 | all-reduce | flops 16 | bytes 128 | tf_op jit(solution)/shard_map/psum | solution.py:89
  20.6 3.2 all-to-all-start.3
  25.6 1.1 slice_reduce_fusion.3
  32.3 2.1 copy.94
  34.4 2.0 copy.97
  37.5 1.5 copy.95
  38.9 2.3 copy.96
  41.9 4.8 all-to-all-start
  46.6 1.3 fusion.182
  47.9 4.0 all-to-all-done
  52.5 3.2 all-to-all-start.2
  55.8 1.3 fusion.173
  57.1 1.4 fusion.174
  58.5 1.4 fusion.183
  59.8 1.2 all-to-all-done.2
  61.7 3.6 all-to-all-start.1
  65.2 1.3 fusion.179
  66.6 1.4 fusion.180
  67.9 2.6 all-to-all-done.1
  70.6 1.4 fusion.176
  72.0 1.4 fusion.177
  73.3 1.4 convolution_convert_fusion
  74.7 1.4 convolution_convert_fusion.1
  80.5 108.2 %all-reduce.1 = (f32[4,4]{1,0:T(4,128)S(1)}, f32[4,4]{1,0:T(4,128)S(1)}, f32[4,4]{1,0:T(4,128)S(1)}, f32[4,4]{1,0:T(4,128)S(1)}) all-reduce(f32[4,4]{1,0:T(4,128)S(1)} %get-tuple-element.78, f32[4,4]{1,0:T(4,128)S(1)} %get-tuple-element.125, f32[4,4]{1,0:T(4,128)S(1)} %get-tuple-element.123, ...), channel_id=1, replica_groups=mesh['seq'=64,'tp'=4] {'seq'}, use_global_device_ids=true, to_apply=%region_40.41 | all-reduce | flops 64 | bytes 512 | tf_op jit(solution)/shard_map/pmax | solution.py:129
  188.9 1.7 fusion.12
  190.6 1.7 fusion.14
  193.8 231.8 %all-reduce = (f32[4,4]{1,0:T(4,128)S(1)}, f32[4,256]{1,0:T(4,128)S(1)}, f32[4,4]{1,0:T(4,128)S(1)}, f32[4,256]{1,0:T(4,128)S(1)}, f32[4,4]{1,0:T(4,128)S(1)}, /...) all-reduce(f32[4,4]{1,0:T(4,128)S(1)} %get-tuple-element.70, ...), channel_id=1, replica_groups=mesh['seq'=64,'tp'=4] {'seq'}, use_global_device_ids=true, to_apply=%region_44.45 | all-reduce | flops 4160 | bytes 33280 | tf_op jit(solution)/shard_map/psum | solution.py:131
  427.8 1.2 convolution_bitcast_fusion.5
  429.2 1.2 convolution_bitcast_fusion.4
  430.9 1.2 convolution_bitcast_fusion.6
  432.6 1.1 convolution_bitcast_fusion.7
  435.8 44.6 %reduce-scatter.33.cloned.1.call-done = f32[256,4]{1,0:T(8,128)} async-done(((f32[1024,4]{1,0:T(8,128)}), f32[256,4]{1,0:T(8,128)}) %reduce-scatter.33.cloned.1.call-update) | async-done | bytes 4112
  481.3 25.3 %reduce-scatter.37.cloned.1.call-done = f32[256,4]{1,0:T(8,128)} async-done(((f32[1024,4]{1,0:T(8,128)}), f32[256,4]{1,0:T(8,128)}) %reduce-scatter.37.cloned.1.call-update) | async-done | bytes 4112
  507.6 25.3 %reduce-scatter.29.cloned.1.call-done = f32[256,4]{1,0:T(8,128)} async-done(((f32[1024,4]{1,0:T(8,128)}), f32[256,4]{1,0:T(8,128)}) %reduce-scatter.29.cloned.1.call-update) | async-done | bytes 4112
  533.9 25.2 %reduce-scatter.25.cloned.1.call-done = f32[256,4]{1,0:T(8,128)} async-done(((f32[1024,4]{1,0:T(8,128)}), f32[256,4]{1,0:T(8,128)}) %reduce-scatter.25.cloned.1.call-update) | async-done | bytes 4112
  560.3 8.4 %all-reduce.2 = (f32[4]{0:T(128)S(1)}, f32[4]{0:T(128)S(1)}, f32[4]{0:T(128)S(1)}, f32[4]{0:T(128)S(1)}) all-reduce(f32[4]{0:T(128)S(1)} %get-tuple-element.158, f32[4]{0:T(128)S(1)} %get-tuple-element.54, f32[4]{0:T(128)S(1)} %get-tuple-element.156, f32[4]{0:T(128)S(1)} %get-tuple-element.47), channel_id=1, replica_groups=mesh['seq'=64,'tp'=4] {'tp'}, use_global_device_ids=true, to_apply=%region_48.49 | all-reduce | flops 16 | bytes 128 | tf_op jit(solution)/shard_map/psum | solution.py:159
  568.9 10.4 %all_gather.12 = bf16[4,1024]{1,0:T(4,128)(2,1)S(1)} all-gather(bf16[4,256]{1,0:T(4,128)(2,1)S(1)} %get-tuple-element.130), channel_id=1, replica_groups=mesh['seq'=64,'tp'=4] {'tp'}, dimensions={1}, use_global_device_ids=true | all-gather | bytes 10240 | tf_op jit(solution)/shard_map/all_gather | solution.py:164
  579.2 10.4 %all_gather.13 = bf16[4,1024]{1,0:T(4,128)(2,1)S(1)} all-gather(bf16[4,256]{1,0:T(4,128)(2,1)S(1)} %get-tuple-element.131), channel_id=1, replica_groups=mesh['seq'=64,'tp'=4] {'tp'}, dimensions={1}, use_global_device_ids=true | all-gather | bytes 10240 | tf_op jit(solution)/shard_map/all_gather | solution.py:164
  589.7 10.5 %all_gather.14 = bf16[4,1024]{1,0:T(4,128)(2,1)S(1)} all-gather(bf16[4,256]{1,0:T(4,128)(2,1)S(1)} %get-tuple-element.132), channel_id=1, replica_groups=mesh['seq'=64,'tp'=4] {'tp'}, dimensions={1}, use_global_device_ids=true | all-gather | bytes 10240 | tf_op jit(solution)/shard_map/all_gather | solution.py:164
  601.4 4.1 convolution_bitcast_fusion.3
  605.6 4.1 convolution_bitcast_fusion.2
  609.6 4.1 convolution_bitcast_fusion.1
  613.7 10.5 %all_gather.15 = bf16[4,1024]{1,0:T(4,128)(2,1)S(1)} all-gather(bf16[4,256]{1,0:T(4,128)(2,1)S(1)} %get-tuple-element.133), channel_id=1, replica_groups=mesh['seq'=64,'tp'=4] {'tp'}, dimensions={1}, use_global_device_ids=true | all-gather | bytes 10240 | tf_op jit(solution)/shard_map/all_gather | solution.py:164
  625.0 4.1 convolution_bitcast_fusion
  629.1 1.2 reduce-scatter.27.cloned.1.call-done
  631.3 25.2 %reduce-scatter.31.cloned.1.call-done = f32[256,4]{1,0:T(8,128)} async-done(((f32[1024,4]{1,0:T(8,128)}), f32[256,4]{1,0:T(8,128)}) %reduce-scatter.31.cloned.1.call-update) | async-done | bytes 4112
  657.4 25.3 %reduce-scatter.35.cloned.1.call-done = f32[256,4]{1,0:T(8,128)} async-done(((f32[1024,4]{1,0:T(8,128)}), f32[256,4]{1,0:T(8,128)}) %reduce-scatter.35.cloned.1.call-update) | async-done | bytes 4112
  683.7 25.3 %reduce-scatter.39.cloned.1.call-done = f32[256,4]{1,0:T(8,128)} async-done(((f32[1024,4]{1,0:T(8,128)}), f32[256,4]{1,0:T(8,128)}) %reduce-scatter.39.cloned.1.call-update) | async-done | bytes 4112
  (197 shorter events, 35.5 us)
Async XLA Ops:
  7.2 593.1 %copy-start = (bf16[1024,1024]{1,0:T(8,128)(2,1)S(1)}, bf16[1024,1024]{1,0:T(8,128)(2,1)}, u32[]{:S(2)}) copy-start(bf16[1024,1024]{1,0:T(8,128)(2,1)} %param.26) | copy-start | bytes 6291460
  7.2 29.2 %copy-start.5 = (bf16[1024,256]{1,0:T(8,128)(2,1)S(1)}, bf16[1024,256]{1,0:T(8,128)(2,1)}, u32[]{:S(2)}) copy-start(bf16[1024,256]{1,0:T(8,128)(2,1)} %param.24) | copy-start | bytes 1572868
  20.6 20.7 %all-to-all-start.3 = ((bf16[4,4,256]{2,1,0:T(4,128)(2,1)}), bf16[4,4,256]{2,1,0:T(4,128)(2,1)S(1)}, u32[]{:S(2)}, u32[]{:S(2)}) async-start(bf16[4,4,256]{2,1,0:T(4,128)(2,1)} %stack.124), calls=%async_computation.3 | async-start | bytes 16384 | tf_op jit(solution)/shard_map/all_to_all | solution.py:95
  41.9 10.1 %all-to-all-start = ((bf16[4,4,256]{2,1,0:T(4,128)(2,1)}), bf16[4,4,256]{2,1,0:T(4,128)(2,1)S(1)}, u32[]{:S(2)}, u32[]{:S(2)}) async-start(bf16[4,4,256]{2,1,0:T(4,128)(2,1)} %stack.50), calls=%async_computation | async-start | bytes 16384 | tf_op jit(solution)/shard_map/all_to_all | solution.py:95
  52.5 8.5 %all-to-all-start.2 = ((bf16[4,4,256]{2,1,0:T(4,128)(2,1)}), bf16[4,4,256]{2,1,0:T(4,128)(2,1)S(1)}, u32[]{:S(2)}, u32[]{:S(2)}) async-start(bf16[4,4,256]{2,1,0:T(4,128)(2,1)} %stack.58), calls=%async_computation.2 | async-start | bytes 16384 | tf_op jit(solution)/shard_map/all_to_all | solution.py:95
  61.7 8.9 %all-to-all-start.1 = ((bf16[4,4,256]{2,1,0:T(4,128)(2,1)}), bf16[4,4,256]{2,1,0:T(4,128)(2,1)S(1)}, u32[]{:S(2)}, u32[]{:S(2)}) async-start(bf16[4,4,256]{2,1,0:T(4,128)(2,1)} %stack.52), calls=%async_computation.1 | async-start | bytes 16384 | tf_op jit(solution)/shard_map/all_to_all | solution.py:95
  65.2 415.1 %reduce-scatter.33.cloned.1.call-start = ((), (), s32[]{:S(2)}) async-start(), calls=%async_computation.16 | async-start | bytes 655360
  70.6 5.5 copy-start.2
  188.7 3.6 copy-start.4
  190.6 236.2 %copy-start.3 = (bf16[1024,256]{0,1:T(8,128)(2,1)S(1)}, bf16[1024,256]{0,1:T(8,128)(2,1)}, u32[]{:S(2)}) copy-start(bf16[1024,256]{0,1:T(8,128)(2,1)} %copy.99) | copy-start | bytes 1572868
  190.6 237.2 %copy-start.1 = (bf16[256,1024]{1,0:T(8,128)(2,1)S(1)}, bf16[256,1024]{1,0:T(8,128)(2,1)}, u32[]{:S(2)}) copy-start(bf16[256,1024]{1,0:T(8,128)(2,1)} %param.25) | copy-start | bytes 1572868
  429.0 77.6 %reduce-scatter.37.cloned.1.call-start = ((), (), s32[]{:S(2)}) async-start(), calls=%async_computation.18 | async-start | bytes 655360
  430.9 102.1 %reduce-scatter.29.cloned.1.call-start = ((), (), s32[]{:S(2)}) async-start(), calls=%async_computation.14 | async-start | bytes 655360
  432.5 126.5 %reduce-scatter.25.cloned.1.call-start = ((), (), s32[]{:S(2)}) async-start(), calls=%async_computation.12 | async-start | bytes 655360
  434.5 195.8 %reduce-scatter.27.cloned.1.call-start = ((), (), s32[]{:S(2)}) async-start(), calls=%async_computation.13 | async-start | bytes 655360
  605.5 50.9 %reduce-scatter.31.cloned.1.call-start = ((), (), s32[]{:S(2)}) async-start(), calls=%async_computation.15 | async-start | bytes 655360
  624.2 58.5 %reduce-scatter.35.cloned.1.call-start = ((), (), s32[]{:S(2)}) async-start(), calls=%async_computation.17 | async-start | bytes 655360
  624.9 84.1 %reduce-scatter.39.cloned.1.call-start = ((), (), s32[]{:S(2)}) async-start(), calls=%async_computation.19 | async-start | bytes 655360
Sparse Core Ops, SparseCore 0:
  429.1 51.1 reduce-scatter.32
  482.9 23.7 reduce-scatter.36
  509.2 23.7 reduce-scatter.28
  535.3 23.7 reduce-scatter.24
  605.6 24.6 reduce-scatter.26
  632.7 23.7 reduce-scatter.30
  658.9 23.7 reduce-scatter.34
  685.2 23.7 reduce-scatter.38
